TPU v7x, 32 devices: a whole 2x2x4 slice. The times are simulated.
32 devices in a mesh: groups: 2 (over x), dom: 16 (over z, y, core).
Axes of the slice: x: 2, y: 2, z: 4, core: 2. Of those that a mesh axis runs over, the one named last changes fastest.
Arguments:
- points: bfloat16 [655360, 256], P(('groups', 'dom')), parts along dimension 0
- counts: int32 [32], P(('groups', 'dom')), parts along dimension 0, may hold values from 0 to 160, as said below
- destination: int32 [5120], P(('groups', 'dom')), parts along dimension 0, may hold values from -1 to 1279, as said below
- proj_weight: bfloat16 [256, 256], replicated, may hold values from -0.375 to 0.375
- proj_bias: float32 [256], replicated, may hold values from -3 to 3
- slice_weight: bfloat16 [32, 32], replicated, may hold values from -1 to 1
- softness_matrix: bfloat16 [32], replicated, may hold values from -1 to 1
- token_qkv_weight: float32 [3, 32, 32], replicated, may hold values from -1 to 1
- out_weight: bfloat16 [256, 256], replicated, may hold values from -0.375 to 0.375
- out_bias: float32 [256], replicated, may hold values from -2 to 2
Outputs:
- result: bfloat16 [327680, 256], P(('groups', 'dom')), parts along dimension 0
There are 2 independent parts, one for each index of `groups`. A program takes and returns all parts, laid end to end along the dimension named above; an argument that names none is the same for every part. Nothing has to cross between parts.
Inputs may be any that keep to these rules, and one draw needn't show every extreme that they name: `counts`: the entries sum to 1280; each is at most 160, and some owner holds exactly 160. `destination`: slot t of owner o holds a placed tile index when t < counts[o], else -1. Placed indices of live slots are distinct and cover all 1280 placed tiles; placed tile p lies on device p // 80. At most 10 live tiles of one owner go to one device, and this is reached in every draw.
All inputs are finite; a program needn't handle non-finite values.
Results may differ from a plain program's by a relative error of at most 0.0014.
The roundings to bfloat16 on the way count: a program that leaves them out, or rounds other values in their place, can miss the bound.
Values may be sent and summed in bfloat16 or wider, within the bound.
A program may use at most 128 MiB of HBM per device.

v0:
```python
import jax
import jax.numpy as jnp
from jax import lax
from jax.sharding import PartitionSpec as P

MODEL_WIDTH = 256
FOCUS_GROUPS = 8
HEAD_FEATURES = 32
PARTITION_TALLY = 32
TILE = 128
LAND = 80


def normalize(values):
    widened = values.astype(jnp.float32)
    centred = widened - jnp.mean(widened, axis=-1, keepdims=True)
    spread = jnp.mean(centred * centred, axis=-1, keepdims=True)
    return (centred * lax.rsqrt(spread + 1e-05)).astype(jnp.bfloat16)


def encode(values, proj_weight, proj_bias, slice_weight, softness_matrix):
    tally_per_line = values.shape[0]
    normed = normalize(values)
    mapped_surface_vectors = (
        jnp.dot(normed, proj_weight, preferred_element_type=jnp.float32) + proj_bias
    ).astype(jnp.bfloat16)
    slice_full = jnp.kron(
        jnp.eye(FOCUS_GROUPS, dtype=jnp.float32), slice_weight.astype(jnp.float32)
    ).astype(jnp.bfloat16)
    softness_broadcast = jnp.kron(
        jnp.eye(FOCUS_GROUPS, dtype=jnp.float32), softness_matrix.astype(jnp.float32)[:, None]
    ).astype(jnp.bfloat16)
    partition_logits = jnp.dot(
        mapped_surface_vectors, slice_full, preferred_element_type=jnp.float32
    )
    partition_softness = 0.5 + jax.nn.softplus(
        jnp.dot(mapped_surface_vectors, softness_broadcast, preferred_element_type=jnp.float32)
    )
    tempered_logits = (
        partition_logits.reshape(tally_per_line, FOCUS_GROUPS, PARTITION_TALLY)
        / partition_softness[:, :, None]
    )
    raised = jnp.exp(tempered_logits)
    slice_assignment = (raised / jnp.sum(raised, axis=-1, keepdims=True)).reshape(
        tally_per_line, FOCUS_GROUPS * PARTITION_TALLY
    )
    return (mapped_surface_vectors, slice_assignment.astype(jnp.bfloat16))


def global_slices(mapped_surface_vectors, slice_assignment, live_mask):
    tally_per_line = mapped_surface_vectors.shape[0]
    masked_scores = slice_assignment * live_mask[:, None]
    numerator_sums = jnp.einsum(
        "lzi,lzt->zit",
        masked_scores.reshape(tally_per_line, FOCUS_GROUPS, PARTITION_TALLY),
        mapped_surface_vectors.reshape(tally_per_line, FOCUS_GROUPS, HEAD_FEATURES),
        preferred_element_type=jnp.float32,
    )
    denom = jnp.sum(masked_scores, axis=0, dtype=jnp.float32)
    return lax.psum((numerator_sums, denom), "dom")


def mix_slices(numerator_sums, denom, token_qkv_weight):
    slice_tokens = numerator_sums / (
        denom.reshape(FOCUS_GROUPS, PARTITION_TALLY)[:, :, None] + 1e-05
    )
    highest_precision = lax.Precision.HIGHEST
    slice_query = jnp.einsum(
        "ijt,tk->ijk", slice_tokens, token_qkv_weight[0], precision=highest_precision
    )
    slice_keys = jnp.einsum(
        "ijt,tk->ijk", slice_tokens, token_qkv_weight[1], precision=highest_precision
    )
    slice_values = jnp.einsum(
        "ijt,tk->ijk", slice_tokens, token_qkv_weight[2], precision=highest_precision
    )
    scores = jnp.einsum(
        "hme,hne->hmn", slice_query, slice_keys, precision=highest_precision
    ) * HEAD_FEATURES ** (-0.5)
    raised = jnp.exp(scores)
    attend = raised / jnp.sum(raised, axis=-1, keepdims=True)
    return jnp.einsum("hmn,hne->hme", attend, slice_values, precision=highest_precision).astype(
        jnp.bfloat16
    )


def decode(slice_assignment, mixed_tokens, out_weight, out_bias):
    tally_per_line = slice_assignment.shape[0]
    unslice_tokens = (
        jnp.einsum(
            "sxw,xwk->sxk",
            slice_assignment.reshape(tally_per_line, FOCUS_GROUPS, PARTITION_TALLY),
            mixed_tokens,
            preferred_element_type=jnp.float32,
        )
        .reshape(tally_per_line, MODEL_WIDTH)
        .astype(jnp.bfloat16)
    )
    return (
        jnp.dot(unslice_tokens, out_weight, preferred_element_type=jnp.float32) + out_bias
    ).astype(jnp.bfloat16)


def to_landing(own_tiles, destination, own_count):
    slot_total = own_tiles.shape[0]
    per_peer = slot_total // lax.axis_size("dom")
    tile_index = jnp.arange(slot_total, dtype=jnp.int32)
    live_tiles = tile_index < own_count
    target_device = jnp.where(live_tiles, destination // LAND, -1)
    target_slot = jnp.where(live_tiles, destination % LAND, -1)
    earlier = (
        (target_device[:, None] == target_device[None, :])
        & live_tiles[None, :]
        & (tile_index[None, :] < tile_index[:, None])
    )
    peer_rank = jnp.sum(earlier.astype(jnp.int32), axis=1)
    send_place = target_device * per_peer + peer_rank
    matches = live_tiles[None, :] & (send_place[None, :] == tile_index[:, None])
    source_tile = jnp.sum(jnp.where(matches, tile_index[None, :], 0), axis=1)
    filled = jnp.any(matches, axis=1)
    outgoing = jnp.where(
        filled[:, None, None], own_tiles[source_tile], jnp.zeros_like(own_tiles[:1])
    )
    slot_label = jnp.where(filled, target_slot[source_tile], -1).astype(jnp.bfloat16)
    arrived, arrived_label = (
        lax.all_to_all(outgoing, "dom", split_axis=0, concat_axis=0, tiled=True),
        lax.all_to_all(slot_label, "dom", split_axis=0, concat_axis=0, tiled=True),
    )
    label_index = arrived_label.astype(jnp.float32).astype(jnp.int32)
    picks = label_index[None, :] == jnp.arange(LAND, dtype=jnp.int32)[:, None]
    chosen = jnp.sum(jnp.where(picks, tile_index[None, :], 0), axis=1)
    return arrived[chosen]


def on_device(
    points,
    counts,
    destination,
    proj_weight,
    proj_bias,
    slice_weight,
    softness_matrix,
    token_qkv_weight,
    out_weight,
    out_bias,
):
    own_count = counts[0]
    slot_total = points.shape[0] // TILE
    placed = to_landing(
        points.reshape(slot_total, TILE, MODEL_WIDTH), destination, own_count
    ).reshape(LAND * TILE, MODEL_WIDTH)
    live_mask = jnp.ones((LAND * TILE,), jnp.bfloat16)
    mapped_surface_vectors, slice_assignment = encode(
        placed, proj_weight, proj_bias, slice_weight, softness_matrix
    )
    numerator_sums, denom = global_slices(mapped_surface_vectors, slice_assignment, live_mask)
    mixed_tokens = mix_slices(numerator_sums, denom, token_qkv_weight)
    return decode(slice_assignment, mixed_tokens, out_weight, out_bias)


def solution(mesh):
    placed = (
        P(("groups", "dom"), None),
        P(("groups", "dom")),
        P(("groups", "dom")),
        P(),
        P(),
        P(),
        P(),
        P(),
        P(),
        P(),
    )
    return jax.shard_map(
        on_device, mesh=mesh, in_specs=placed, out_specs=P(("groups", "dom"), None), check_vma=False
    )
```

profile of v0, /device:TPU:0, one launch (start us, length us, event | category | flops | bytes accessed | tf_op | source)
XLA Modules:
  0.0 379.6 jit_solution(10969523679690145396)
XLA Ops:
  0.7 0.7 fusion.26
  1.9 1.6 gather_fusion.1
  3.5 0.7 convert_element_type.122
  4.2 7.4 %all-to-all-start.1 = ((bf16[16,10,1]{1,2,0:T(2,128)(2,1)}), bf16[16,10,1]{1,2,0:T(2,128)(2,1)S(1)}, u32[]{:S(2)}, u32[]{:S(2)}) async-start(bf16[16,10,1]{1,2,0:T(2,128)(2,1)} %convert_element_type.122), calls=%async_computation.1 | async-start | bytes 16384 | tf_op jit(solution)/shard_map/all_to_all | solution.py:127
  11.6 11.4 %gather_fusion = bf16[160,128,256]{2,1,0:T(8,128)(2,1)} fusion(bf16[160,128,256]{2,1,0:T(8,128)(2,1)} %bitcast.68, s32[1024]{0:T(1024)S(1)} %pad_clamp_fusion.1), kind=kCustom, calls=%fused_computation | custom fusion | bytes 20972160 | tf_op jit(solution)/shard_map/gather | solution.py:122
  23.1 10.0 %broadcast_select_fusion = bf16[160,128,256]{2,1,0:T(8,128)(2,1)} fusion(bf16[160,128,256]{2,1,0:T(8,128)(2,1)} %gather_fusion, pred[160]{0:T(512)(128)(4,1)S(1)} %fusion.11), kind=kLoop, calls=%fused_computation.16 | loop fusion | flops 5242880 | bytes 20971680 | tf_op jit(solution)/shard_map/jit(_where)/select_n | solution.py:121
  33.1 6.2 %all-to-all-start = ((bf16[160,128,256]{2,1,0:T(8,128)(2,1)}), bf16[160,128,256]{2,1,0:T(8,128)(2,1)}, u32[]{:S(2)}, u32[]{:S(2)}) async-start(bf16[160,128,256]{2,1,0:T(8,128)(2,1)} %broadcast_select_fusion), calls=%async_computation | async-start | bytes 20971520 | tf_op jit(solution)/shard_map/all_to_all | solution.py:126
  39.7 0.4 convert_element_type.111
  40.4 185.9 %all-to-all-done = bf16[160,128,256]{2,1,0:T(8,128)(2,1)} async-done(((bf16[160,128,256]{2,1,0:T(8,128)(2,1)}), bf16[160,128,256]{2,1,0:T(8,128)(2,1)}, u32[]{:S(2)}, u32[]{:S(2)}) %all-to-all-start) | async-done | bytes 10485792 | tf_op jit(solution)/shard_map/all_to_all | solution.py:126
  226.3 9.7 %gather_fusion.2 = bf16[80,128,256]{2,1,0:T(8,128)(2,1)} fusion(bf16[160,128,256]{2,1,0:T(8,128)(2,1)} %all-to-all-done, s32[1024]{0:T(1024)S(1)} %pad_clamp_fusion), kind=kCustom, calls=%fused_computation.2 | custom fusion | bytes 10486080 | tf_op jit(solution)/shard_map/gather | solution.py:132
  236.0 4.1 %convert_reduce_fusion.1 = f32[80,128]{1,0:T(8,128)S(1)} fusion(bf16[80,128,256]{2,1,0:T(8,128)(2,1)} %gather_fusion.2), kind=kLoop, calls=%fused_computation.18 | loop fusion | flops 5232640 | bytes 5283840 | tf_op jit(solution)/shard_map/reduce_sum | solution.py:16
  240.1 3.3 multiply_reduce_fusion
  243.4 5.7 %fusion.4 = bf16[10240,256]{1,0:T(8,128)(2,1)S(1)} fusion(bf16[80,128,256]{2,1,0:T(8,128)(2,1)S(1)} %copy-done.2, f32[10240]{0:T(1024)S(1)} %rsqrt_bitcast_fusion, f32[10240]{0:T(1024)S(1)} %get-tuple-element.7), kind=kLoop, calls=%fused_computation.12 | loop fusion | flops 10485760 | bytes 10567680 | tf_op jit(solution)/shard_map/convert_element_type | solution.py:18
  249.1 1.6 fusion
  250.8 2.3 copy-done.3
  253.1 0.8 fusion.8
  254.0 7.2 %convert_reduce_fusion = (f32[8,32]{1,0:T(8,128)S(1)}, bf16[10240,8,32]{0,2,1:T(8,128)(2,1)}) fusion(bf16[8,32,256]{2,1,0:T(8,128)(2,1)S(1)} %bitcast.70, bf16[10240,256]{0,1:T(8,128)(2,1)} %copy-done.3, f32[10240,8]{0,1:T(8,128)S(1)} %fusion.8), kind=kOutput, calls=%fused_computation.13 | convolution fusion | flops 1355366144 | bytes 10945536 | tf_op jit(solution)/shard_map/div | solution.py:44
  261.2 5.5 %fusion.33 = f32[8,32,32]{2,1,0:T(8,128)S(1)} fusion(bf16[10240,8,32]{0,2,1:T(8,128)(2,1)} %get-tuple-element.12, bf16[10240,8,32]{0,2,1:T(8,128)(2,1)} %bitcast.67), kind=kOutput, calls=%fused_computation.70 | convolution fusion | flops 167772160 | bytes 10518528 | tf_op jit(solution)/shard_map/lzi,lzt->zit/dot_general | solution.py:53
  266.8 102.9 %all-reduce = (f32[8,32,32]{2,1,0:T(8,128)S(1)}, f32[256]{0:T(256)S(1)}) all-reduce(f32[8,32,32]{2,1,0:T(8,128)S(1)} %fusion.33, f32[256]{0:T(256)S(1)} %reduce_sum.87), channel_id=1, replica_groups=mesh['groups'=2,'dom'=16] {'dom'}, use_global_device_ids=true, to_apply=%region_7.8 | all-reduce | flops 8448 | bytes 67584 | tf_op jit(solution)/shard_map/psum | solution.py:60
  369.8 0.3 fusion.18
  370.7 0.3 fusion.7
  371.1 0.4 convolution_convert_fusion.1
  371.5 4.1 %convolution_convert_fusion = bf16[8,32,10240]{2,1,0:T(8,128)(2,1)S(1)} fusion(bf16[8,32,32]{2,1,0:T(8,128)(2,1)S(1)} %convolution_convert_fusion.1, bf16[10240,8,32]{0,2,1:T(8,128)(2,1)} %get-tuple-element.12), kind=kOutput, calls=%fused_computation.7 | convolution fusion | flops 170393600 | bytes 10502144 | tf_op jit(solution)/shard_map/sxw,xwk->sxk/dot_general | solution.py:90
  375.6 3.9 %fusion.1 = bf16[10240,256]{1,0:T(8,128)(2,1)} fusion(bf16[10240,256]{0,1:T(8,128)(2,1)S(1)} %bitcast.69, bf16[256,256]{1,0:T(8,128)(2,1)S(1)} %copy-done.7, f32[256]{0:T(256)S(1)} %copy-done.9), kind=kOutput, calls=%fused_computation.6 | convolution fusion | flops 1347420160 | bytes 10617856 | tf_op jit(solution)/shard_map/dot_general | solution.py:100
  (47 shorter events, 2.1 us)
Async XLA Ops:
  0.0 249.1 %copy-start = (bf16[256,256]{1,0:T(8,128)(2,1)S(1)}, bf16[256,256]{1,0:T(8,128)(2,1)}, u32[]{:S(2)}) copy-start(bf16[256,256]{1,0:T(8,128)(2,1)} %param.13) | copy-start | bytes 393220
  4.2 28.9 %all-to-all-start.1 = ((bf16[16,10,1]{1,2,0:T(2,128)(2,1)}), bf16[16,10,1]{1,2,0:T(2,128)(2,1)S(1)}, u32[]{:S(2)}, u32[]{:S(2)}) async-start(bf16[16,10,1]{1,2,0:T(2,128)(2,1)} %convert_element_type.122), calls=%async_computation.1 | async-start | bytes 16384 | tf_op jit(solution)/shard_map/all_to_all | solution.py:127
  33.1 6.3 %copy-start.6 = (bf16[32]{0:T(256)(128)(2,1)S(1)}, bf16[32]{0:T(256)(128)(2,1)}, u32[]{:S(2)}) copy-start(bf16[32]{0:T(256)(128)(2,1)} %param.16) | copy-start | bytes 196
  33.1 6.4 %copy-start.4 = (bf16[32,32]{1,0:T(8,128)(2,1)S(1)}, bf16[32,32]{1,0:T(8,128)(2,1)}, u32[]{:S(2)}) copy-start(bf16[32,32]{1,0:T(8,128)(2,1)} %param.15) | copy-start | bytes 6148
  33.1 193.3 %all-to-all-start = ((bf16[160,128,256]{2,1,0:T(8,128)(2,1)}), bf16[160,128,256]{2,1,0:T(8,128)(2,1)}, u32[]{:S(2)}, u32[]{:S(2)}) async-start(bf16[160,128,256]{2,1,0:T(8,128)(2,1)} %broadcast_select_fusion), calls=%async_computation | async-start | bytes 20971520 | tf_op jit(solution)/shard_map/all_to_all | solution.py:126
  236.0 4.1 %copy-start.2 = (bf16[80,128,256]{2,1,0:T(8,128)(2,1)S(1)}, bf16[80,128,256]{2,1,0:T(8,128)(2,1)}, u32[]{:S(2)}) copy-start(bf16[80,128,256]{2,1,0:T(8,128)(2,1)} %gather_fusion.2) | copy-start | bytes 15728644
  243.4 5.7 %copy-start.5 = (f32[256]{0:T(256)S(1)}, f32[256]{0:T(256)}, u32[]{:S(2)}) copy-start(f32[256]{0:T(256)} %param.14) | copy-start | bytes 3076
  250.8 2.4 copy-start.3
  261.2 108.6 %copy-start.8 = (f32[3,32,32]{2,1,0:T(8,128)S(1)}, f32[3,32,32]{2,1,0:T(8,128)}, u32[]{:S(2)}) copy-start(f32[3,32,32]{2,1,0:T(8,128)} %param.17) | copy-start | bytes 36868
  371.5 4.1 %copy-start.7 = (bf16[256,256]{1,0:T(8,128)(2,1)S(1)}, bf16[256,256]{1,0:T(8,128)(2,1)}, u32[]{:S(2)}) copy-start(bf16[256,256]{1,0:T(8,128)(2,1)} %param.18) | copy-start | bytes 393220
  371.5 4.1 %copy-start.9 = (f32[256]{0:T(256)S(1)}, f32[256]{0:T(256)}, u32[]{:S(2)}) copy-start(f32[256]{0:T(256)} %param.19) | copy-start | bytes 3076
  375.6 4.0 %copy-start.1 = (bf16[256,256]{1,0:T(8,128)(2,1)S(1)}, bf16[256,256]{1,0:T(8,128)(2,1)}, u32[]{:S(2)}) copy-start(bf16[256,256]{1,0:T(8,128)(2,1)} %param.13) | copy-start | bytes 393220
where the time goes:
time: 380 us
  waiting for transfers between devices  186 us (49%)
  blocking collectives  103 us (27%)
  local copies, waits for them, and re-layouts  26.7 us (7%)
  matrix products  24.9 us (7%)
  other arithmetic  24.6 us (6%)
  starting transfers between devices  13.6 us (4%)
    all_to_all x1, waiting for transfers between devices, to_landing(): lax.all_to_all(outgoing, 'dom', split_axis=0, concat_axis=0, tiled=True)  186 us
    psum x1, blocking collectives, global_slices(): return lax.psum((numerator_sums, denom), 'dom')  103 us
    gather x1, local copies, waits for them, and re-layouts, to_landing(): own_tiles[source_tile]  11.4 us
    select_n x1, other arithmetic, to_landing(): jnp.where(filled[:, None, None], own_tiles[source_tile], jnp.zeros_like(o...  9.98 us
    gather x1, local copies, waits for them, and re-layouts, to_landing(): return arrived[chosen]  9.68 us
  transfers between devices with their start and end apart: 2, of which 1 were waited for; matrix products, arithmetic and copies ran while one was open for 6% of the time, Pallas kernels for 0%

commit v1 on v0

v1 whole, which is shorter than its diff:
```python
import functools

import jax
import jax.numpy as jnp
from jax import lax
from jax.experimental import pallas as pl
from jax.experimental.pallas import tpu as pltpu
from jax.sharding import PartitionSpec as P

WIDTH = 256
HEADS = 8
FEAT = 32
TILE = 128
LAND = 80
LABEL_ROWS = 16
HALF = 128
MESH = pl.DeviceIdType.MESH
HIGHEST = lax.Precision.HIGHEST
F32 = jnp.float32
BF16 = jnp.bfloat16


def gather_kernel(n, per_peer, order, points, out, hold, in_sem, out_sem):
    def load(k, _):
        def one(t, _):
            s = k * per_peer + t
            pltpu.make_async_copy(points.at[order[s]], hold.at[s], in_sem.at[k]).start()
            return 0

        return lax.fori_loop(0, per_peer, one, 0)

    lax.fori_loop(0, n, load, 0)

    def store(k, _):
        part = pl.ds(k * per_peer, per_peer)
        pltpu.make_async_copy(points.at[pl.ds(0, per_peer)], hold.at[part], in_sem.at[k]).wait()
        pltpu.make_async_copy(hold.at[part], out.at[part], out_sem.at[k]).start()
        return 0

    lax.fori_loop(0, n, store, 0)

    def finish(k, _):
        part = pl.ds(k * per_peer, per_peer)
        pltpu.make_async_copy(hold.at[part], out.at[part], out_sem.at[k]).wait()
        return 0

    lax.fori_loop(0, n, finish, 0)


def encode_rows(x, live, wp, bp, ws, wt, ones):
    x = jnp.where(live, x.astype(F32), 0.0)
    centred = x - jnp.sum(x, axis=-1, keepdims=True) * (1.0 / WIDTH)
    spread = jnp.sum(centred * centred, axis=-1, keepdims=True) * (1.0 / WIDTH)
    normed = (centred * lax.rsqrt(spread + 1e-05)).astype(BF16)
    proj = (jnp.dot(normed, wp, preferred_element_type=F32) + bp).astype(BF16)
    logits = jnp.dot(proj, ws, preferred_element_type=F32)
    soft = jnp.dot(proj, wt, preferred_element_type=F32)
    temper = 0.5 + (jnp.maximum(soft, 0.0) + jnp.log1p(jnp.exp(-jnp.abs(soft))))
    raised = jnp.exp(logits / temper)
    total = jnp.dot(raised, ones, preferred_element_type=F32, precision=HIGHEST)
    weights = (raised / total).astype(BF16)
    return proj, weights


def move_kernel(
    n, per_peer, step_tiles, outgoing, labels, wp, bp, ws, wt, ones, weights_out, labels_out, stats_out,
    arrived, held, arrived_lab, numer, denom, sums, inbox,
    send_sem, recv_sem, lab_send, lab_recv, own_sem, w_sem, red_send, red_recv,
):
    me = lax.axis_index("dom")
    barrier = pltpu.get_barrier_semaphore()
    for k in range(1, n):
        pl.semaphore_signal(barrier, inc=1, device_id={"dom": lax.rem(me + k, n)}, device_id_type=MESH)
    pl.semaphore_wait(barrier, n - 1)

    def lab_copy(k, peer):
        return pltpu.make_async_remote_copy(
            src_ref=labels.at[peer], dst_ref=arrived_lab.at[k], send_sem=lab_send.at[k],
            recv_sem=lab_recv.at[k], device_id={"dom": peer}, device_id_type=MESH,
        )

    def tile_copy(k, peer):
        return pltpu.make_async_remote_copy(
            src_ref=outgoing.at[peer], dst_ref=arrived.at[k], send_sem=send_sem.at[k],
            recv_sem=recv_sem.at[k], device_id={"dom": peer}, device_id_type=MESH,
        )

    own = pltpu.make_async_copy(outgoing.at[me], arrived.at[0], own_sem.at[0])
    own.start()
    own_lab = pltpu.make_async_copy(labels.at[me], arrived_lab.at[0], own_sem.at[1])
    own_lab.start()
    for k in range(1, n):
        lab_copy(k, lax.rem(me + k, n)).start()
    for k in range(1, n):
        tile_copy(k, lax.rem(me + k, n)).start()

    numer[...] = jnp.zeros_like(numer)
    denom[...] = jnp.zeros_like(denom)
    rows = step_tiles * TILE

    def block(k):
        def step(s, _):
            t0 = s * step_tiles
            at = pl.ds(pl.multiple_of(t0 * TILE, TILE), rows)
            x = arrived[k, at, :]
            live = jnp.concatenate(
                [
                    jnp.broadcast_to(arrived_lab[k, pl.ds(t0 + j, 1), :][:, :1], (TILE, 1))
                    for j in range(step_tiles)
                ],
                axis=0,
            ) >= 0
            proj, weights = encode_rows(x, live, wp[...], bp[...], ws[...], wt[...], ones[...])
            weights = jnp.where(live, weights.astype(F32), 0.0).astype(BF16)
            held[k, at, :] = weights
            numer[...] += lax.dot_general(
                weights, proj, (((0,), (0,)), ((), ())), preferred_element_type=F32
            )
            denom[...] += jnp.sum(weights.astype(F32).reshape(rows // 8, 8, WIDTH), axis=0)
            return 0

        lax.fori_loop(0, per_peer // step_tiles, step, 0)
        pltpu.make_async_copy(held.at[k], weights_out.at[k], w_sem.at[k]).start()

    own.wait()
    own_lab.wait()
    block(0)

    def from_peer(k, _):
        peer = lax.rem(me + k, n)
        lab_copy(k, peer).wait_recv()
        tile_copy(k, peer).wait_recv()
        block(k)
        return 0

    lax.fori_loop(1, n, from_peer, 0)

    lane_head = lax.broadcasted_iota(jnp.int32, (FEAT, HALF), 1) // FEAT
    for a in range(2):
        acc = jnp.zeros((FEAT, HALF), F32)
        for j in range(4):
            part = numer[pl.ds((a * 4 + j) * FEAT, FEAT), pl.ds(a * HALF, HALF)]
            acc = acc + jnp.where(lane_head == j, part, 0.0)
        sums[0, pl.ds(a * FEAT, FEAT), :] = acc
        total = jnp.sum(denom[:, pl.ds(a * HALF, HALF)], axis=0, keepdims=True)
        sums[0, pl.ds(2 * FEAT + a * 8, 8), :] = jnp.broadcast_to(total, (8, HALF))

    level, bit = 0, 1
    while bit < n:
        partner = me + bit - 2 * bit * (me // bit % 2)
        swap = pltpu.make_async_remote_copy(
            src_ref=sums.at[level], dst_ref=inbox.at[level], send_sem=red_send.at[level],
            recv_sem=red_recv.at[level], device_id={"dom": partner}, device_id_type=MESH,
        )
        swap.start()
        swap.wait()
        sums[level + 1] = sums[level] + inbox[level]
        level, bit = level + 1, bit * 2
    stats_out[...] = sums[level]
    labels_out[...] = arrived_lab[...]

    def finish(k, _):
        peer = lax.rem(me + k, n)
        lab_copy(k, peer).wait_send()
        tile_copy(k, peer).wait_send()
        return 0

    lax.fori_loop(1, n, finish, 0)

    def drain(k, _):
        pltpu.make_async_copy(held.at[k], weights_out.at[k], w_sem.at[k]).wait()
        return 0

    lax.fori_loop(0, n, drain, 0)


def mix(stats, qkv, ones):
    row_head = lax.broadcasted_iota(jnp.int32, (HALF, HALF), 0) // FEAT
    lane_head = lax.broadcasted_iota(jnp.int32, (HALF, HALF), 1) // FEAT
    same = row_head == lane_head
    blocks = []
    for a in range(2):
        numer = stats[a * FEAT:(a + 1) * FEAT, :]
        row = stats[2 * FEAT + a * 8:2 * FEAT + (a + 1) * 8, :]
        col = jnp.transpose(jnp.broadcast_to(row[:1], (HALF, HALF)))
        spread = jnp.zeros((FEAT, HALF), F32)
        for j in range(4):
            spread = spread + jnp.where(
                lane_head[:FEAT] == j, col[j * FEAT:(j + 1) * FEAT, :], 0.0
            )
        tokens = numer / (spread + 1e-05)
        dot = functools.partial(jnp.dot, preferred_element_type=F32, precision=HIGHEST)
        query, keys, values = (dot(tokens, qkv[i]) for i in range(3))
        spread_keys = jnp.where(same, jnp.concatenate([keys] * 4, axis=0), 0.0)
        scores = lax.dot_general(
            query, spread_keys, (((1,), (1,)), ((), ())), preferred_element_type=F32, precision=HIGHEST
        ) * FEAT ** (-0.5)
        raised = jnp.exp(scores)
        attend = raised / dot(raised, ones)
        spread_values = jnp.where(same, jnp.concatenate([values] * 4, axis=0), 0.0)
        mixed = dot(attend, spread_values)
        blocks.append(jnp.where(same, jnp.concatenate([mixed] * 4, axis=0), 0.0))
    nil = jnp.zeros((HALF, HALF), F32)
    return jnp.concatenate(
        [jnp.concatenate([blocks[0], nil], axis=1), jnp.concatenate([nil, blocks[1]], axis=1)], axis=0
    ).astype(BF16)


def decode_kernel(
    chunks, per_chunk, chosen, weights, stats, qkv, ones, wo, bo, out, held, done, mixed, in_sem, out_sem
):
    def load(c, _):
        def one(t, _):
            p = c * per_chunk + t
            pltpu.make_async_copy(weights.at[chosen[p]], held.at[p], in_sem.at[c]).start()
            return 0

        return lax.fori_loop(0, per_chunk, one, 0)

    lax.fori_loop(0, chunks, load, 0)
    mixed[...] = mix(stats[...], qkv, ones[...])
    rows = per_chunk * TILE

    def step(c, _):
        part = pl.ds(c * per_chunk, per_chunk)
        pltpu.make_async_copy(weights.at[pl.ds(0, per_chunk)], held.at[part], in_sem.at[c]).wait()
        w = held[part].reshape(rows, WIDTH)
        deslice = jnp.dot(w, mixed[...], preferred_element_type=F32).astype(BF16)
        y = (jnp.dot(deslice, wo[...], preferred_element_type=F32) + bo[...]).astype(BF16)
        at = pl.ds(pl.multiple_of(c * rows, rows), rows)
        done[at, :] = y
        pltpu.make_async_copy(done.at[at], out.at[at], out_sem.at[c]).start()
        return 0

    lax.fori_loop(0, chunks, step, 0)

    def finish(c, _):
        at = pl.ds(pl.multiple_of(c * rows, rows), rows)
        pltpu.make_async_copy(done.at[at], out.at[at], out_sem.at[c]).wait()
        return 0

    lax.fori_loop(0, chunks, finish, 0)


def plan(destination, own_count, n):
    slots = destination.shape[0]
    per_peer = slots // n
    index = jnp.arange(slots, dtype=jnp.int32)
    live = index < own_count
    target = jnp.where(live, destination // LAND, -1)
    slot = jnp.where(live, destination % LAND, -1)
    earlier = (target[:, None] == target[None, :]) & live[None, :] & (index[None, :] < index[:, None])
    rank = jnp.sum(earlier.astype(jnp.int32), axis=1)
    place = target * per_peer + rank
    matches = live[None, :] & (place[None, :] == index[:, None])
    source = jnp.sum(jnp.where(matches, index[None, :], 0), axis=1)
    label = jnp.sum(jnp.where(matches, slot[None, :] + 1, 0), axis=1) - 1
    return source, label


def on_device(n, points, counts, destination, wp, bp, slice_weight, softness, qkv, wo, bo):
    slots = points.shape[0] // TILE
    per_peer = slots // n
    any_spec = pl.BlockSpec(memory_space=pl.ANY)
    vmem = pl.BlockSpec(memory_space=pltpu.VMEM)
    source, label = plan(destination, counts[0], n)
    outgoing = pl.pallas_call(
        functools.partial(gather_kernel, n, per_peer),
        out_shape=jax.ShapeDtypeStruct((slots, TILE, WIDTH), BF16),
        grid_spec=pltpu.PrefetchScalarGridSpec(
            num_scalar_prefetch=1, grid=(), in_specs=[any_spec], out_specs=any_spec,
            scratch_shapes=[
                pltpu.VMEM((slots, TILE, WIDTH), BF16),
                pltpu.SemaphoreType.DMA((n,)), pltpu.SemaphoreType.DMA((n,)),
            ],
        ),
        compiler_params=pltpu.CompilerParams(vmem_limit_bytes=60 << 20),
        name="gather",
    )(source, points.reshape(slots, TILE, WIDTH))

    rows = per_peer * TILE
    labels = jnp.broadcast_to(
        jnp.pad(label.reshape(n, per_peer), ((0, 0), (0, LABEL_ROWS - per_peer)), constant_values=-1)[
            :, :, None
        ],
        (n, LABEL_ROWS, HALF),
    )
    eye = jnp.eye(HEADS, dtype=F32)
    ws = jnp.kron(eye, slice_weight.astype(F32)).astype(BF16)
    wt = jnp.kron(eye, jnp.broadcast_to(softness.astype(F32)[:, None], (FEAT, FEAT))).astype(BF16)
    ones = jnp.kron(eye, jnp.ones((FEAT, FEAT), F32))
    step_tiles = 2 if per_peer % 2 == 0 else 1
    levels = (n - 1).bit_length()
    stat_rows = 2 * FEAT + 16
    weights, arrived_lab, stats = pl.pallas_call(
        functools.partial(move_kernel, n, per_peer, step_tiles),
        out_shape=(
            jax.ShapeDtypeStruct((n, rows, WIDTH), BF16),
            jax.ShapeDtypeStruct((n, LABEL_ROWS, HALF), jnp.int32),
            jax.ShapeDtypeStruct((stat_rows, HALF), F32),
        ),
        in_specs=[any_spec, any_spec] + [vmem] * 5,
        out_specs=(any_spec, vmem, vmem),
        scratch_shapes=[
            pltpu.VMEM((n, rows, WIDTH), BF16),
            pltpu.VMEM((n, rows, WIDTH), BF16),
            pltpu.VMEM((n, LABEL_ROWS, HALF), jnp.int32),
            pltpu.VMEM((WIDTH, WIDTH), F32),
            pltpu.VMEM((8, WIDTH), F32),
            pltpu.VMEM((levels + 1, stat_rows, HALF), F32),
            pltpu.VMEM((levels, stat_rows, HALF), F32),
            pltpu.SemaphoreType.DMA((n,)), pltpu.SemaphoreType.DMA((n,)),
            pltpu.SemaphoreType.DMA((n,)), pltpu.SemaphoreType.DMA((n,)),
            pltpu.SemaphoreType.DMA((2,)), pltpu.SemaphoreType.DMA((n,)),
            pltpu.SemaphoreType.DMA((levels,)), pltpu.SemaphoreType.DMA((levels,)),
        ],
        compiler_params=pltpu.CompilerParams(
            collective_id=0, has_side_effects=True, vmem_limit_bytes=60 << 20
        ),
        name="move",
    )(outgoing.reshape(n, rows, WIDTH), labels, wp, bp.reshape(1, WIDTH), ws, wt, ones)

    slot_label = arrived_lab[:, :per_peer, 0].reshape(slots)
    index = jnp.arange(slots, dtype=jnp.int32)
    picks = slot_label[None, :] == jnp.arange(LAND, dtype=jnp.int32)[:, None]
    chosen = jnp.sum(jnp.where(picks, index[None, :], 0), axis=1)
    qkv_wide = jax.vmap(lambda w: jnp.kron(jnp.eye(4, dtype=F32), w))(qkv)
    per_chunk = 8
    chunks = LAND // per_chunk
    return pl.pallas_call(
        functools.partial(decode_kernel, chunks, per_chunk),
        out_shape=jax.ShapeDtypeStruct((LAND * TILE, WIDTH), BF16),
        grid_spec=pltpu.PrefetchScalarGridSpec(
            num_scalar_prefetch=1, grid=(), in_specs=[any_spec] + [vmem] * 5, out_specs=any_spec,
            scratch_shapes=[
                pltpu.VMEM((LAND, TILE, WIDTH), BF16),
                pltpu.VMEM((LAND * TILE, WIDTH), BF16),
                pltpu.VMEM((WIDTH, WIDTH), BF16),
                pltpu.SemaphoreType.DMA((chunks,)), pltpu.SemaphoreType.DMA((chunks,)),
            ],
        ),
        compiler_params=pltpu.CompilerParams(vmem_limit_bytes=60 << 20),
        name="decode",
    )(
        chosen, weights.reshape(slots, TILE, WIDTH), stats, qkv_wide, ones[:HALF, :HALF], wo,
        bo.reshape(1, WIDTH),
    )


def solution(mesh):
    spec = P(("groups", "dom"))
    wide = P(("groups", "dom"), None)
    return jax.shard_map(
        functools.partial(on_device, mesh.shape["dom"]),
        mesh=mesh,
        in_specs=(wide, spec, spec) + (P(),) * 7,
        out_specs=wide,
        check_vma=False,
    )
```

time: 380 us -> 341 us (0.90)
  Pallas kernels: 0 us -> 330 us
  waiting for transfers between devices: 186 us -> 0 us
  blocking collectives: 103 us -> 0 us
  matrix products: 24.9 us -> 0 us
  local copies, waits for them, and re-layouts: 26.7 us -> 5.3 us
  other arithmetic: 24.6 us -> 3.75 us
  starting transfers between devices: 13.6 us -> 0 us
    pallas_call x0 -> x3, Pallas kernels: none -> 330 us  [the longest x1 308 us: on_device(): pl.pallas_call(functools.partial(move_kernel, n, per_peer, step_tiles), o...]
    all_to_all x2 -> x0, waiting for transfers between devices: 186 us -> none  [the longest x1 186 us: to_landing(): lax.all_to_all(outgoing, 'dom', split_axis=0, concat_axis=0, tiled=True)]
    psum x1 -> x0, blocking collectives: 103 us -> none  [global_slices(): return lax.psum((numerator_sums, denom), 'dom')]
    gather x3 -> x0, local copies, waits for them, and re-layouts: 22.7 us -> none  [the longest x1 11.4 us: to_landing(): own_tiles[source_tile]]
    dot_general x10 -> x0, matrix products: 17.7 us -> none  [the longest x1 5.54 us: global_slices(): jnp.einsum('lzi,lzt->zit', masked_scores.reshape(tally_per_line, FOCUS_GR...]
    all_to_all x2 -> x0, starting transfers between devices: 13.6 us -> none  [the longest x1 7.41 us: to_landing(): lax.all_to_all(slot_label, 'dom', split_axis=0, concat_axis=0, tiled=True)]
    select_n x4 -> x1, other arithmetic: 10.7 us -> 0.69 us  [plan(): target = jnp.where(live, destination // LAND, -1)]
    div x1 -> x0, matrix products: 7.18 us -> none  [encode(): raised / jnp.sum(raised, axis=-1, keepdims=True)]
  transfers between devices with their start and end apart: 2 -> 0, of which waited for: 1 -> 0; matrix products, arithmetic and copies ran while one was open for 6% -> 0% of each run, Pallas kernels for 0% -> 0%
where the time goes in v1:
time: 341 us; the launch traced here: 340 us
  Pallas kernels  330 us (97%)
  local copies, waits for them, and re-layouts  5.3 us (2%)
  other arithmetic  3.75 us (1%)
    pallas_call x1, Pallas kernels, on_device(): pl.pallas_call(functools.partial(move_kernel, n, per_peer, step_tiles), o...  308 us
    pallas_call x1, Pallas kernels, on_device(): pl.pallas_call(functools.partial(gather_kernel, n, per_peer), out_shape=j...  11.2 us
    pallas_call x1, Pallas kernels, on_device(): pl.pallas_call(functools.partial(decode_kernel, chunks, per_chunk), out_s...  10.5 us

profile of v1, /device:TPU:0, one launch (start us, length us, event | category | flops | bytes accessed | tf_op | source)
XLA Modules:
  0.0 339.6 jit_solution(13673519767959249316)
XLA Ops:
  0.7 0.7 fusion.5
  1.4 0.2 convert_reduce_fusion
  1.6 0.7 select_reduce_fusion
  2.3 11.2 %gather.1 = bf16[160,128,256]{2,1,0:T(8,128)(2,1)} custom-call(s32[160]{0:T(256)} %get-tuple-element.12.order, bf16[160,128,256]{2,1,0:T(8,128)(2,1)} %bitcast.14), custom_call_target="tpu_custom_call" | custom-call | tf_op jit(solution)/shard_map/gather/pallas_call | solution.py:267
  13.5 0.0 copy-start.1
  13.5 0.1 sub.14
  13.6 0.7 broadcast_in_dim.68.labels
  14.4 0.1 mul.96
  14.5 0.3 mul.97.ones
  14.9 0.1 mul.98
  14.9 0.3 mul.99
  15.3 0.1 mul.102
  15.4 0.7 multiply_convert_fusion
  16.1 308.0 %move.1 = (bf16[16,1280,256]{2,1,0:T(8,128)(2,1)}, s32[16,16,128]{2,1,0:T(8,128)}, f32[80,128]{1,0:T(8,128)}) custom-call(bf16[16,1280,256]{2,1,0:T(8,128)(2,1)} %bitcast.12, s32[16,16,128]{2,1,0:T(8,128)} %broadcast_in_dim.68.labels, bf16[256,256]{1,0:T(8,128)(2,1)} %wp.1, f32[1,256]{1,0:T(1,128)} %bitcast.15, bf16[256,256]{1,0:T(8,128)(2,1)} %get-tuple-element.14.ws, ...), custom_call_target="tpu_custom_call" | custom-call | tf_op jit(solution)/shard_map/move/pallas_call | solution.py:295
  324.2 1.2 slice_reduce_fusion
  325.4 0.1 eq.67
  325.5 0.7 select_reduce_fusion.2.chosen
  326.2 1.5 slice.8.ones
  327.6 0.1 mul.108
  327.8 0.4 mul.109
  328.1 0.1 mul.105
  328.2 0.2 mul.106
  328.4 0.7 broadcast_multiply_fusion.qkv
  329.1 10.5 %decode.1 = bf16[10240,256]{1,0:T(8,128)(2,1)} custom-call(s32[80]{0:T(128)} %select_reduce_fusion.2.chosen, bf16[160,128,256]{2,1,0:T(8,128)(2,1)} %bitcast.13, f32[80,128]{1,0:T(8,128)} %get-tuple-element.10.stats, f32[3,128,128]{2,1,0:T(8,128)} %broadcast_multiply_fusion.qkv, f32[128,128]{1,0:T(8,128)} %slice.8.ones, bf16[256,256]{1,0:T(8,128)(2,1)} %wo.1, ...), custom_call_target="tpu_custom_call" | custom-call | tf_op jit(solution)/shard_map/decode/pallas_call | solution.py:330
  (14 shorter events, 0.1 us)
Async XLA Ops:
  2.3 12.6 %copy-start.2 = (bf16[32,32]{1,0:T(8,128)(2,1)S(1)}, bf16[32,32]{1,0:T(8,128)(2,1)}, u32[]{:S(2)}) copy-start(bf16[32,32]{1,0:T(8,128)(2,1)} %param.15) | copy-start | bytes 6148
  2.3 13.0 %copy-start.3 = (bf16[32]{0:T(256)(128)(2,1)S(1)}, bf16[32]{0:T(256)(128)(2,1)}, u32[]{:S(2)}) copy-start(bf16[32]{0:T(256)(128)(2,1)} %param.16) | copy-start | bytes 196
  13.5 314.1 %copy-start.1 = (f32[3,32,32]{2,1,0:T(8,128)S(1)}, f32[3,32,32]{2,1,0:T(8,128)}, u32[]{:S(2)}) copy-start(f32[3,32,32]{2,1,0:T(8,128)} %param.17) | copy-start | bytes 36868
  14.9 1.3 copy-start

commit v2 on v1

v2 whole, which is shorter than its diff:
```python
import functools

import jax
import jax.numpy as jnp
from jax import lax
from jax.experimental import pallas as pl
from jax.experimental.pallas import tpu as pltpu
from jax.sharding import PartitionSpec as P

WIDTH = 256
HEADS = 8
FEAT = 32
TILE = 128
LAND = 80
HALF = 128
MESH = pl.DeviceIdType.MESH
HIGHEST = lax.Precision.HIGHEST
F32 = jnp.float32
BF16 = jnp.bfloat16


def split(x):
    high = x.astype(BF16)
    return high, x - high.astype(F32)


def encode_rows(x, wp, bp, ws, wt, spread_ones, ones):
    x = x.astype(F32)
    centred = x - jnp.sum(x, axis=-1, keepdims=True) * (1.0 / WIDTH)
    spread = jnp.sum(centred * centred, axis=-1, keepdims=True) * (1.0 / WIDTH)
    normed = (centred * lax.rsqrt(spread + 1e-05)).astype(BF16)
    dot = functools.partial(jnp.dot, preferred_element_type=F32)
    proj = (dot(normed, wp) + bp).astype(BF16)
    logits = dot(proj, ws)
    soft = dot(proj, wt)
    temper = 0.5 + (jnp.maximum(soft, 0.0) + jnp.log1p(jnp.exp(-jnp.abs(soft))))
    first, rest = split(1.0 / temper)
    second, rest = split(rest)
    scale = dot(first, spread_ones) + (dot(second, spread_ones) + dot(rest.astype(BF16), spread_ones))
    raised = jnp.exp(logits * scale)
    first, rest = split(raised)
    total = dot(first, ones) + dot(rest.astype(BF16), ones)
    return proj, (raised / total).astype(BF16)


def move_kernel(
    n, per_peer, unit, source, label, points, labels, wp, bp, ws, wt, spread_ones, ones, head_ones, qkv,
    wo, bo, result, labels_out,
    held_points, sending, arrived, numer, denom, sums, inbox, mixed,
    point_sem, send_sem, recv_sem, lab_send, lab_recv, own_sem, out_sem, red_send, red_recv,
):
    me = lax.axis_index("dom")
    pieces = per_peer // unit
    rows = unit * TILE
    fetch = pltpu.make_async_copy(points, held_points, point_sem)
    fetch.start()

    def partner(x):
        peer, bit = 0, 1
        while bit < n:
            mine, flip = me // bit % 2, x // bit % 2
            peer = peer + bit * (mine + flip - 2 * mine * flip)
            bit = bit * 2
        return peer

    barrier = pltpu.get_barrier_semaphore()
    for x in range(1, n):
        pl.semaphore_signal(barrier, inc=1, device_id={"dom": partner(x)}, device_id_type=MESH)
    numer[...] = jnp.zeros_like(numer)
    denom[...] = jnp.zeros_like(denom)
    pl.semaphore_wait(barrier, n - 1)

    def lab_copy(x):
        peer = partner(x)
        return pltpu.make_async_remote_copy(
            src_ref=labels.at[peer], dst_ref=labels_out.at[me], send_sem=lab_send.at[x],
            recv_sem=lab_recv.at[x], device_id={"dom": peer}, device_id_type=MESH,
        )

    def piece_copy(x, s):
        at = pl.ds(pl.multiple_of(s * rows, rows), rows)
        return pltpu.make_async_remote_copy(
            src_ref=sending.at[x, at], dst_ref=arrived.at[x, at], send_sem=send_sem.at[x, s],
            recv_sem=recv_sem.at[x, s], device_id={"dom": partner(x)}, device_id_type=MESH,
        )

    def lab_start(x, _):
        lab_copy(x).start()
        return 0

    lax.fori_loop(1, n, lab_start, 0)
    own_lab = pltpu.make_async_copy(labels.at[me], labels_out.at[me], own_sem)
    own_lab.start()
    fetch.wait()

    def compute(x, peer, s):
        first = peer * per_peer + s * unit
        tiles = jnp.concatenate([held_points[source[first + j]] for j in range(unit)], axis=0)
        proj, weights = encode_rows(
            tiles, wp[...], bp[...], ws[...], wt[...], spread_ones[...], ones[...]
        )
        live = jnp.concatenate(
            [jnp.full((TILE, WIDTH), label[first + j], jnp.int32) for j in range(unit)], axis=0
        ) >= 0
        kept = jnp.where(live, weights.astype(F32), 0.0)
        weights = kept.astype(BF16)
        sending[x, pl.ds(pl.multiple_of(s * rows, rows), rows), :] = weights
        numer[...] += lax.dot_general(
            weights, proj, (((0,), (0,)), ((), ())), preferred_element_type=F32
        )
        denom[...] += jnp.sum(kept.reshape(rows // 8, 8, WIDTH), axis=0)

    steps = (n - 1) * pieces

    def encode_step(i, _):
        x = n - 1 - i // pieces
        compute(x, partner(x), i % pieces)

        @pl.when(i > 0)
        def _():
            piece_copy(n - 1 - (i - 1) // pieces, (i - 1) % pieces).start()

        return 0

    lax.fori_loop(0, steps, encode_step, 0)

    def own_step(s, _):
        compute(0, me, s)

        @pl.when(s == 0)
        def _():
            piece_copy(1, pieces - 1).start()

        return 0

    lax.fori_loop(0, pieces, own_step, 0)

    lane_head = lax.broadcasted_iota(jnp.int32, (FEAT, HALF), 1) // FEAT
    for a in range(2):
        acc = jnp.zeros((FEAT, HALF), F32)
        for j in range(4):
            part = numer[pl.ds((a * 4 + j) * FEAT, FEAT), pl.ds(a * HALF, HALF)]
            acc = acc + jnp.where(lane_head == j, part, 0.0)
        sums[0, pl.ds(a * FEAT, FEAT), :] = acc
        total = jnp.sum(denom[:, pl.ds(a * HALF, HALF)], axis=0, keepdims=True)
        sums[0, pl.ds(2 * FEAT + a * 8, 8), :] = jnp.broadcast_to(total, (8, HALF))

    level, bit = 0, 1
    while bit < n:
        swap = pltpu.make_async_remote_copy(
            src_ref=sums.at[level], dst_ref=inbox.at[level], send_sem=red_send.at[level],
            recv_sem=red_recv.at[level], device_id={"dom": partner(bit)}, device_id_type=MESH,
        )
        swap.start()
        swap.wait()
        sums[level + 1] = sums[level] + inbox[level]
        level, bit = level + 1, bit * 2
    mixed[...] = mix(sums[level], qkv, head_ones[...])

    def decode(read, x):
        def one(s, _):
            at = pl.ds(pl.multiple_of(s * rows, rows), rows)
            deslice = jnp.dot(read[x, at, :], mixed[...], preferred_element_type=F32).astype(BF16)
            y = (jnp.dot(deslice, wo[...], preferred_element_type=F32) + bo[...]).astype(BF16)
            arrived[x, at, :] = y
            return 0

        lax.fori_loop(0, pieces, one, 0)
        pltpu.make_async_copy(arrived.at[x], result.at[partner(x)], out_sem.at[x]).start()

    decode(sending, 0)

    def from_peer(i, _):
        x = n - 1 - i

        def one(s, _):
            piece_copy(x, s).wait_recv()
            return 0

        lax.fori_loop(0, pieces, one, 0)
        decode(arrived, x)
        return 0

    lax.fori_loop(0, n - 1, from_peer, 0)

    def finish(x, _):
        def one(s, _):
            piece_copy(x, s).wait_send()
            return 0

        lax.fori_loop(0, pieces, one, 0)
        lab_copy(x).wait()
        return 0

    lax.fori_loop(1, n, finish, 0)
    own_lab.wait()

    def drain(x, _):
        pltpu.make_async_copy(arrived.at[x], result.at[partner(x)], out_sem.at[x]).wait()
        return 0

    lax.fori_loop(0, n, drain, 0)


def mix(stats, qkv, ones):
    row_head = lax.broadcasted_iota(jnp.int32, (HALF, HALF), 0) // FEAT
    lane_head = lax.broadcasted_iota(jnp.int32, (HALF, HALF), 1) // FEAT
    same = row_head == lane_head
    blocks = []
    for a in range(2):
        numer = stats[a * FEAT:(a + 1) * FEAT, :]
        row = stats[2 * FEAT + a * 8:2 * FEAT + (a + 1) * 8, :]
        col = jnp.transpose(jnp.broadcast_to(row[:1], (HALF, HALF)))
        spread = jnp.zeros((FEAT, HALF), F32)
        for j in range(4):
            spread = spread + jnp.where(
                lane_head[:FEAT] == j, col[j * FEAT:(j + 1) * FEAT, :], 0.0
            )
        tokens = numer / (spread + 1e-05)
        dot = functools.partial(jnp.dot, preferred_element_type=F32, precision=HIGHEST)
        query, keys, values = (dot(tokens, qkv[i]) for i in range(3))
        spread_keys = jnp.where(same, jnp.concatenate([keys] * 4, axis=0), 0.0)
        scores = lax.dot_general(
            query, spread_keys, (((1,), (1,)), ((), ())), preferred_element_type=F32, precision=HIGHEST
        ) * FEAT ** (-0.5)
        raised = jnp.exp(scores)
        attend = raised / dot(raised, ones)
        spread_values = jnp.where(same, jnp.concatenate([values] * 4, axis=0), 0.0)
        mixed = dot(attend, spread_values)
        blocks.append(jnp.where(same, jnp.concatenate([mixed] * 4, axis=0), 0.0))
    nil = jnp.zeros((HALF, HALF), F32)
    return jnp.concatenate(
        [jnp.concatenate([blocks[0], nil], axis=1), jnp.concatenate([nil, blocks[1]], axis=1)], axis=0
    ).astype(BF16)


def place_kernel(n, per_peer, chunks, per_chunk, labels, tiles, out, held, in_sem, out_sem):
    def load(k, _):
        def one(t, _):
            slot = labels[k, t]

            @pl.when(slot >= 0)
            def _():
                pltpu.make_async_copy(
                    tiles.at[k * per_peer + t], held.at[slot], in_sem.at[slot // per_chunk]
                ).start()

            return 0

        return lax.fori_loop(0, per_peer, one, 0)

    lax.fori_loop(0, n, load, 0)

    def step(c, _):
        part = pl.ds(c * per_chunk, per_chunk)
        pltpu.make_async_copy(tiles.at[pl.ds(0, per_chunk)], held.at[part], in_sem.at[c]).wait()
        pltpu.make_async_copy(held.at[part], out.at[part], out_sem.at[c]).start()
        return 0

    lax.fori_loop(0, chunks, step, 0)

    def finish(c, _):
        part = pl.ds(c * per_chunk, per_chunk)
        pltpu.make_async_copy(held.at[part], out.at[part], out_sem.at[c]).wait()
        return 0

    lax.fori_loop(0, chunks, finish, 0)


def plan(destination, own_count, n):
    slots = destination.shape[0]
    per_peer = slots // n
    index = jnp.arange(slots, dtype=jnp.int32)
    live = index < own_count
    target = jnp.where(live, destination // LAND, -1)
    slot = jnp.where(live, destination % LAND, -1)
    earlier = (target[:, None] == target[None, :]) & live[None, :] & (index[None, :] < index[:, None])
    rank = jnp.sum(earlier.astype(jnp.int32), axis=1)
    place = target * per_peer + rank
    matches = live[None, :] & (place[None, :] == index[:, None])
    source = jnp.sum(jnp.where(matches, index[None, :], 0), axis=1)
    label = jnp.sum(jnp.where(matches, slot[None, :] + 1, 0), axis=1) - 1
    return source, label


def on_device(n, points, counts, destination, wp, bp, slice_weight, softness, qkv, wo, bo):
    slots = points.shape[0] // TILE
    per_peer = slots // n
    any_spec = pl.BlockSpec(memory_space=pl.ANY)
    vmem = pl.BlockSpec(memory_space=pltpu.VMEM)
    smem = pl.BlockSpec(memory_space=pltpu.SMEM)
    source, label = plan(destination, counts[0], n)
    rows = per_peer * TILE
    labels = jnp.pad(label.reshape(n, 1, per_peer), ((0, 0), (0, 0), (0, HALF - per_peer)))
    eye = jnp.eye(HEADS, dtype=F32)
    ws = jnp.kron(eye, slice_weight.astype(F32)).astype(BF16)
    narrow = jnp.eye(HEADS, HALF, dtype=F32)
    wt = jnp.kron(narrow, softness.astype(F32)[:, None])
    wt = wt.reshape(WIDTH, HALF).astype(BF16)
    spread_ones = jnp.kron(narrow, jnp.ones((FEAT, 1), F32)).reshape(WIDTH, HALF).T.astype(BF16)
    ones = jnp.kron(eye, jnp.ones((FEAT, FEAT), F32))
    qkv_wide = jax.vmap(lambda w: jnp.kron(jnp.eye(4, dtype=F32), w))(qkv)
    unit = 2 if per_peer % 2 == 0 else 1
    pieces = per_peer // unit
    levels = (n - 1).bit_length()
    stat_rows = 2 * FEAT + 16
    dma = pltpu.SemaphoreType.DMA
    tiles, arrived_lab = pl.pallas_call(
        functools.partial(move_kernel, n, per_peer, unit),
        out_shape=(
            jax.ShapeDtypeStruct((n, rows, WIDTH), BF16),
            jax.ShapeDtypeStruct((n, 1, HALF), jnp.int32),
        ),
        in_specs=[smem, smem, any_spec, any_spec] + [vmem] * 10,
        out_specs=(any_spec, any_spec),
        scratch_shapes=[
            pltpu.VMEM((slots, TILE, WIDTH), BF16),
            pltpu.VMEM((n, rows, WIDTH), BF16),
            pltpu.VMEM((n, rows, WIDTH), BF16),
            pltpu.VMEM((WIDTH, WIDTH), F32),
            pltpu.VMEM((8, WIDTH), F32),
            pltpu.VMEM((levels + 1, stat_rows, HALF), F32),
            pltpu.VMEM((levels, stat_rows, HALF), F32),
            pltpu.VMEM((WIDTH, WIDTH), BF16),
            dma, dma((n, pieces)), dma((n, pieces)), dma((n,)), dma((n,)), dma, dma((n,)),
            dma((levels,)), dma((levels,)),
        ],
        compiler_params=pltpu.CompilerParams(
            collective_id=0, has_side_effects=True, vmem_limit_bytes=60 << 20
        ),
        name="move",
    )(
        source, label, points.reshape(slots, TILE, WIDTH), labels, wp, bp.reshape(1, WIDTH), ws, wt,
        spread_ones, ones.astype(BF16), ones[:HALF, :HALF], qkv_wide, wo, bo.reshape(1, WIDTH),
    )

    per_chunk = 8
    chunks = LAND // per_chunk
    placed = pl.pallas_call(
        functools.partial(place_kernel, n, per_peer, chunks, per_chunk),
        out_shape=jax.ShapeDtypeStruct((LAND, TILE, WIDTH), BF16),
        grid_spec=pltpu.PrefetchScalarGridSpec(
            num_scalar_prefetch=1, grid=(), in_specs=[any_spec], out_specs=any_spec,
            scratch_shapes=[pltpu.VMEM((LAND, TILE, WIDTH), BF16), dma((chunks,)), dma((chunks,))],
        ),
        compiler_params=pltpu.CompilerParams(vmem_limit_bytes=60 << 20),
        name="place",
    )(arrived_lab.reshape(n, HALF), tiles.reshape(slots, TILE, WIDTH))
    return placed.reshape(LAND * TILE, WIDTH)


def solution(mesh):
    spec = P(("groups", "dom"))
    wide = P(("groups", "dom"), None)
    return jax.shard_map(
        functools.partial(on_device, mesh.shape["dom"]),
        mesh=mesh,
        in_specs=(wide, spec, spec) + (P(),) * 7,
        out_specs=wide,
        check_vma=False,
    )
```

time: 341 us -> 313 us (0.918)
  Pallas kernels: 330 us -> 302 us
    pallas_call x3 -> x2, Pallas kernels: 330 us -> 302 us  [the longest x1 296 us: on_device(): pl.pallas_call(functools.partial(move_kernel, n, per_peer, unit), out_sha...]
where the time goes in v2:
time: 313 us
  Pallas kernels  302 us (96%)
  local copies, waits for them, and re-layouts  5.87 us (2%)
  other arithmetic  3.78 us (1%)
    pallas_call x1, Pallas kernels, on_device(): pl.pallas_call(functools.partial(move_kernel, n, per_peer, unit), out_sha...  296 us

profile of v2, /device:TPU:0, one launch (start us, length us, event | category | flops | bytes accessed | tf_op | source)
XLA Modules:
  0.0 312.6 jit_solution(8124617209919450325)
XLA Ops:
  0.7 0.7 fusion.6
  1.4 0.2 convert_reduce_fusion
  1.6 0.7 select_reduce_fusion
  2.3 0.0 copy-start
  2.3 0.7 mul.126
  2.9 0.1 mul.127
  3.0 0.1 sub.14
  3.1 0.6 pad.4.labels
  3.7 0.7 multiply_convert_fusion.1.wt
  4.5 0.7 copy.15
  5.2 0.1 mul.130
  5.3 0.2 mul.131
  5.5 0.9 mul.133
  6.4 0.4 mul.134
  6.8 0.7 broadcast_multiply_fusion.qkv
  7.5 0.1 mul.119
  7.6 0.3 mul.120
  7.9 0.6 slice.4.head_ones
  8.5 0.8 mul.121
  9.3 0.3 mul.122
  9.6 0.8 fusion.8
  10.4 0.0 copy-done
  10.4 296.5 %move.1 = (bf16[16,1280,256]{2,1,0:T(8,128)(2,1)}, s32[16,1,128]{2,1,0:T(1,128)}) custom-call(s32[160]{0:T(256)} %get-tuple-element.10.source, s32[160]{0:T(256)} %copy-done, bf16[160,128,256]{2,1,0:T(8,128)(2,1)} %bitcast.19, s32[16,1,128]{2,1,0:T(1,128)} %pad.4.labels, bf16[256,256]{1,0:T(8,128)(2,1)} %wp.1, f32[1,256]{1,0:T(1,128)} %bitcast.25, ...), custom_call_target="tpu_custom_call" | custom-call | tf_op jit(solution)/shard_map/move/pallas_call | solution.py:308
  306.8 5.8 %place.1 = bf16[80,128,256]{2,1,0:T(8,128)(2,1)} custom-call(s32[16,128]{1,0:T(8,128)} %bitcast.24, bf16[160,128,256]{2,1,0:T(8,128)(2,1)} %bitcast.20), custom_call_target="tpu_custom_call" | custom-call | tf_op jit(solution)/shard_map/place/pallas_call | solution.py:339
  (7 shorter events, 0.0 us)
Async XLA Ops:
  2.3 8.1 %copy-start = (s32[160]{0:T(256)}, s32[160]{0:T(256)S(1)}, u32[]{:S(2)}) copy-start(s32[160]{0:T(256)S(1)} %broadcast_add_fusion.label) | copy-start | bytes 1924

commit v3 on v2

--- a/solution.py
+++ b/solution.py
@@ -43,10 +43,38 @@
     return proj, (raised / total).astype(BF16)
 
 
+def diagonal(block, times):
+    wide = jnp.concatenate([block] * times, axis=1)
+    full = jnp.concatenate([wide] * times, axis=0)
+    size = times * FEAT
+    row = lax.broadcasted_iota(jnp.int32, (size, size), 0) // FEAT
+    lane = lax.broadcasted_iota(jnp.int32, (size, size), 1) // FEAT
+    return jnp.where(row == lane, full, 0.0)
+
+
+def build(slice_weight, softness, qkv_small, ws, wt, spread_ones, ones, head_ones, qkv):
+    ws[...] = diagonal(slice_weight[...].astype(F32), HEADS).astype(BF16)
+    for i in range(3):
+        qkv[i] = diagonal(qkv_small[i], 4)
+    unity = jnp.ones((FEAT, FEAT), F32)
+    ones[...] = diagonal(unity, HEADS).astype(BF16)
+    head_ones[...] = diagonal(unity, 4)
+    row = lax.broadcasted_iota(jnp.int32, (HALF, WIDTH), 0)
+    lane = lax.broadcasted_iota(jnp.int32, (HALF, WIDTH), 1) // FEAT
+    spread_ones[...] = jnp.where(row == lane, 1.0, 0.0).astype(BF16)
+    flat = jnp.concatenate([softness[...].astype(F32)] * 4, axis=1)
+    tall = jnp.transpose(jnp.broadcast_to(flat, (HALF, HALF)))
+    tall = jnp.concatenate([tall, tall], axis=0)
+    row = lax.broadcasted_iota(jnp.int32, (WIDTH, HALF), 0) // FEAT
+    lane = lax.broadcasted_iota(jnp.int32, (WIDTH, HALF), 1)
+    wt[...] = jnp.where(row == lane, tall, 0.0).astype(BF16)
+
+
 def move_kernel(
-    n, per_peer, unit, source, label, points, labels, wp, bp, ws, wt, spread_ones, ones, head_ones, qkv,
+    n, per_peer, unit, source, label, points, labels, wp, bp, slice_weight, softness, qkv_small,
     wo, bo, result, labels_out,
     held_points, sending, arrived, numer, denom, sums, inbox, mixed,
+    ws, wt, spread_ones, ones, head_ones, qkv,
     point_sem, send_sem, recv_sem, lab_send, lab_recv, own_sem, out_sem, red_send, red_recv,
 ):
     me = lax.axis_index("dom")
@@ -68,7 +96,15 @@
         pl.semaphore_signal(barrier, inc=1, device_id={"dom": partner(x)}, device_id_type=MESH)
     numer[...] = jnp.zeros_like(numer)
     denom[...] = jnp.zeros_like(denom)
+    build(slice_weight, softness, qkv_small, ws, wt, spread_ones, ones, head_ones, qkv)
     pl.semaphore_wait(barrier, n - 1)
+
+    def order(i):
+        quarter = n // 4
+        near = lax.rem(i, 2) * 2 * quarter
+        early = 3 * quarter + i // 2 - near
+        late = jnp.where(i < 3 * quarter, i, n - 1 - i)
+        return jnp.where(i < 2 * quarter, early, late)
 
     def lab_copy(x):
         peer = partner(x)
@@ -111,14 +147,15 @@
         denom[...] += jnp.sum(kept.reshape(rows // 8, 8, WIDTH), axis=0)
 
     steps = (n - 1) * pieces
+    held_from = (n - 1) * (pieces - 1)
 
     def encode_step(i, _):
-        x = n - 1 - i // pieces
-        compute(x, partner(x), i % pieces)
-
-        @pl.when(i > 0)
+        x = order(i % (n - 1))
+        compute(x, partner(x), i // (n - 1))
+
+        @pl.when((i > 0) & (i <= held_from))
         def _():
-            piece_copy(n - 1 - (i - 1) // pieces, (i - 1) % pieces).start()
+            piece_copy(order((i - 1) % (n - 1)), (i - 1) // (n - 1)).start()
 
         return 0
 
@@ -126,11 +163,6 @@
 
     def own_step(s, _):
         compute(0, me, s)
-
-        @pl.when(s == 0)
-        def _():
-            piece_copy(1, pieces - 1).start()
-
         return 0
 
     lax.fori_loop(0, pieces, own_step, 0)
@@ -145,8 +177,12 @@
         total = jnp.sum(denom[:, pl.ds(a * HALF, HALF)], axis=0, keepdims=True)
         sums[0, pl.ds(2 * FEAT + a * 8, 8), :] = jnp.broadcast_to(total, (8, HALF))
 
-    level, bit = 0, 1
-    while bit < n:
+    def release(i, _):
+        piece_copy(order(i - held_from), pieces - 1).start()
+        return 0
+
+    level, bit = 0, n // 2
+    while bit > 0:
         swap = pltpu.make_async_remote_copy(
             src_ref=sums.at[level], dst_ref=inbox.at[level], send_sem=red_send.at[level],
             recv_sem=red_recv.at[level], device_id={"dom": partner(bit)}, device_id_type=MESH,
@@ -154,34 +190,35 @@
         swap.start()
         swap.wait()
         sums[level + 1] = sums[level] + inbox[level]
-        level, bit = level + 1, bit * 2
+        level, bit = level + 1, bit // 2
+        if level == max(1, (n - 1).bit_length() - 2):
+            lax.fori_loop(held_from, steps, release, 0)
     mixed[...] = mix(sums[level], qkv, head_ones[...])
 
-    def decode(read, x):
-        def one(s, _):
-            at = pl.ds(pl.multiple_of(s * rows, rows), rows)
-            deslice = jnp.dot(read[x, at, :], mixed[...], preferred_element_type=F32).astype(BF16)
-            y = (jnp.dot(deslice, wo[...], preferred_element_type=F32) + bo[...]).astype(BF16)
-            arrived[x, at, :] = y
-            return 0
-
-        lax.fori_loop(0, pieces, one, 0)
-        pltpu.make_async_copy(arrived.at[x], result.at[partner(x)], out_sem.at[x]).start()
-
-    decode(sending, 0)
+    def out_copy(x, s):
+        at = pl.ds(pl.multiple_of(s * rows, rows), rows)
+        return pltpu.make_async_copy(arrived.at[x, at], result.at[partner(x), at], out_sem.at[x, s])
+
+    def decode(read, x, s):
+        at = pl.ds(pl.multiple_of(s * rows, rows), rows)
+        deslice = jnp.dot(read[x, at, :], mixed[...], preferred_element_type=F32).astype(BF16)
+        y = (jnp.dot(deslice, wo[...], preferred_element_type=F32) + bo[...]).astype(BF16)
+        arrived[x, at, :] = y
+        out_copy(x, s).start()
+
+    def decode_own(s, _):
+        decode(sending, 0, s)
+        return 0
+
+    lax.fori_loop(0, pieces, decode_own, 0)
 
     def from_peer(i, _):
-        x = n - 1 - i
-
-        def one(s, _):
-            piece_copy(x, s).wait_recv()
-            return 0
-
-        lax.fori_loop(0, pieces, one, 0)
-        decode(arrived, x)
-        return 0
-
-    lax.fori_loop(0, n - 1, from_peer, 0)
+        x, s = order(i % (n - 1)), i // (n - 1)
+        piece_copy(x, s).wait_recv()
+        decode(arrived, x, s)
+        return 0
+
+    lax.fori_loop(0, steps, from_peer, 0)
 
     def finish(x, _):
         def one(s, _):
@@ -195,11 +232,11 @@
     lax.fori_loop(1, n, finish, 0)
     own_lab.wait()
 
-    def drain(x, _):
-        pltpu.make_async_copy(arrived.at[x], result.at[partner(x)], out_sem.at[x]).wait()
-        return 0
-
-    lax.fori_loop(0, n, drain, 0)
+    def drain(i, _):
+        out_copy(i // pieces, i % pieces).wait()
+        return 0
+
+    lax.fori_loop(0, n * pieces, drain, 0)
 
 
 def mix(stats, qkv, ones):
@@ -292,14 +329,6 @@
     source, label = plan(destination, counts[0], n)
     rows = per_peer * TILE
     labels = jnp.pad(label.reshape(n, 1, per_peer), ((0, 0), (0, 0), (0, HALF - per_peer)))
-    eye = jnp.eye(HEADS, dtype=F32)
-    ws = jnp.kron(eye, slice_weight.astype(F32)).astype(BF16)
-    narrow = jnp.eye(HEADS, HALF, dtype=F32)
-    wt = jnp.kron(narrow, softness.astype(F32)[:, None])
-    wt = wt.reshape(WIDTH, HALF).astype(BF16)
-    spread_ones = jnp.kron(narrow, jnp.ones((FEAT, 1), F32)).reshape(WIDTH, HALF).T.astype(BF16)
-    ones = jnp.kron(eye, jnp.ones((FEAT, FEAT), F32))
-    qkv_wide = jax.vmap(lambda w: jnp.kron(jnp.eye(4, dtype=F32), w))(qkv)
     unit = 2 if per_peer % 2 == 0 else 1
     pieces = per_peer // unit
     levels = (n - 1).bit_length()
@@ -311,7 +340,7 @@
             jax.ShapeDtypeStruct((n, rows, WIDTH), BF16),
             jax.ShapeDtypeStruct((n, 1, HALF), jnp.int32),
         ),
-        in_specs=[smem, smem, any_spec, any_spec] + [vmem] * 10,
+        in_specs=[smem, smem, any_spec, any_spec] + [vmem] * 7,
         out_specs=(any_spec, any_spec),
         scratch_shapes=[
             pltpu.VMEM((slots, TILE, WIDTH), BF16),
@@ -322,7 +351,13 @@
             pltpu.VMEM((levels + 1, stat_rows, HALF), F32),
             pltpu.VMEM((levels, stat_rows, HALF), F32),
             pltpu.VMEM((WIDTH, WIDTH), BF16),
-            dma, dma((n, pieces)), dma((n, pieces)), dma((n,)), dma((n,)), dma, dma((n,)),
+            pltpu.VMEM((WIDTH, WIDTH), BF16),
+            pltpu.VMEM((WIDTH, HALF), BF16),
+            pltpu.VMEM((HALF, WIDTH), BF16),
+            pltpu.VMEM((WIDTH, WIDTH), BF16),
+            pltpu.VMEM((HALF, HALF), F32),
+            pltpu.VMEM((3, HALF, HALF), F32),
+            dma, dma((n, pieces)), dma((n, pieces)), dma((n,)), dma((n,)), dma, dma((n, pieces)),
             dma((levels,)), dma((levels,)),
         ],
         compiler_params=pltpu.CompilerParams(
@@ -330,8 +365,8 @@
         ),
         name="move",
     )(
-        source, label, points.reshape(slots, TILE, WIDTH), labels, wp, bp.reshape(1, WIDTH), ws, wt,
-        spread_ones, ones.astype(BF16), ones[:HALF, :HALF], qkv_wide, wo, bo.reshape(1, WIDTH),
+        source, label, points.reshape(slots, TILE, WIDTH), labels, wp, bp.reshape(1, WIDTH),
+        slice_weight, softness.reshape(1, FEAT), qkv, wo, bo.reshape(1, WIDTH),
     )
 
     per_chunk = 8

time: 313 us -> 258 us (0.82)
  Pallas kernels: 302 us -> 254 us
  local copies, waits for them, and re-layouts: 5.87 us -> 0.7 us
    pallas_call x1, Pallas kernels: 296 us -> 249 us  [on_device(): pl.pallas_call(functools.partial(move_kernel, n, per_peer, unit), out_sha...]
    mul x12 -> x0, local copies, waits for them, and re-layouts: 4.54 us -> none  [the longest x4 1.55 us: on_device(): qkv_wide = jax.vmap(lambda w: jnp.kron(jnp.eye(4, dtype=F32), w))(qkv)]
where the time goes in v3:
time: 258 us; the launch traced here: 257 us
  Pallas kernels  254 us (98%)
    pallas_call x1, Pallas kernels, on_device(): pl.pallas_call(functools.partial(move_kernel, n, per_peer, unit), out_sha...  249 us
    pallas_call x1, Pallas kernels, on_device(): pl.pallas_call(functools.partial(place_kernel, n, per_peer, chunks, per_c...  5.63 us

profile of v3, /device:TPU:0, one launch (start us, length us, event | category | flops | bytes accessed | tf_op | source)
XLA Modules:
  0.0 257.4 jit_solution(12551900939284227183)
XLA Ops:
  0.7 0.7 fusion.3
  1.4 0.2 convert_reduce_fusion
  1.6 0.7 select_reduce_fusion
  2.2 0.0 copy-start
  2.2 0.1 sub.14
  2.3 0.6 pad.4.labels
  2.9 0.0 copy-done
  2.9 248.8 %move.1 = (bf16[16,1280,256]{2,1,0:T(8,128)(2,1)}, s32[16,1,128]{2,1,0:T(1,128)}) custom-call(s32[160]{0:T(256)} %get-tuple-element.10.source, s32[160]{0:T(256)} %copy-done, bf16[160,128,256]{2,1,0:T(8,128)(2,1)} %bitcast.11, s32[16,1,128]{2,1,0:T(1,128)} %pad.4.labels, bf16[256,256]{1,0:T(8,128)(2,1)} %wp.1, f32[1,256]{1,0:T(1,128)} %bitcast.15, ...), custom_call_target="tpu_custom_call" | custom-call | tf_op jit(solution)/shard_map/move/pallas_call | solution.py:337
  251.8 5.6 %place.1 = bf16[80,128,256]{2,1,0:T(8,128)(2,1)} custom-call(s32[16,128]{1,0:T(8,128)} %bitcast.14, bf16[160,128,256]{2,1,0:T(8,128)(2,1)} %bitcast.12), custom_call_target="tpu_custom_call" | custom-call | tf_op jit(solution)/shard_map/place/pallas_call | solution.py:374
  (3 shorter events, 0.0 us)
Async XLA Ops:
  2.2 0.7 copy-start

commit v4 on v3

--- a/solution.py
+++ b/solution.py
@@ -147,7 +147,7 @@
         denom[...] += jnp.sum(kept.reshape(rows // 8, 8, WIDTH), axis=0)
 
     steps = (n - 1) * pieces
-    held_from = (n - 1) * (pieces - 1)
+    held_from = max(0, (n - 1) * (pieces - 1) - n // 2)
 
     def encode_step(i, _):
         x = order(i % (n - 1))
@@ -178,7 +178,7 @@
         sums[0, pl.ds(2 * FEAT + a * 8, 8), :] = jnp.broadcast_to(total, (8, HALF))
 
     def release(i, _):
-        piece_copy(order(i - held_from), pieces - 1).start()
+        piece_copy(order(i % (n - 1)), i // (n - 1)).start()
         return 0
 
     level, bit = 0, n // 2

time: 258 us -> 258 us (level)
  no operation moved by 1% of the time
where the time goes in v4:
time: 258 us; the launch traced here: 257 us
  Pallas kernels  254 us (98%)
    pallas_call x1, Pallas kernels, on_device(): pl.pallas_call(functools.partial(move_kernel, n, per_peer, unit), out_sha...  249 us
    pallas_call x1, Pallas kernels, on_device(): pl.pallas_call(functools.partial(place_kernel, n, per_peer, chunks, per_c...  5.47 us

profile of v4, /device:TPU:0, one launch (start us, length us, event | category | flops | bytes accessed | tf_op | source)
XLA Modules:
  0.0 257.3 jit_solution(11552961973503735672)
XLA Ops:
  0.7 0.7 fusion.3
  1.4 0.2 convert_reduce_fusion
  1.6 0.7 select_reduce_fusion
  2.2 0.0 copy-start
  2.2 0.1 sub.14
  2.3 0.6 pad.4.labels
  2.9 0.0 copy-done
  2.9 248.9 %move.1 = (bf16[16,1280,256]{2,1,0:T(8,128)(2,1)}, s32[16,1,128]{2,1,0:T(1,128)}) custom-call(s32[160]{0:T(256)} %get-tuple-element.10.source, s32[160]{0:T(256)} %copy-done, bf16[160,128,256]{2,1,0:T(8,128)(2,1)} %bitcast.11, s32[16,1,128]{2,1,0:T(1,128)} %pad.4.labels, bf16[256,256]{1,0:T(8,128)(2,1)} %wp.1, f32[1,256]{1,0:T(1,128)} %bitcast.15, ...), custom_call_target="tpu_custom_call" | custom-call | tf_op jit(solution)/shard_map/move/pallas_call | solution.py:337
  251.8 5.5 %place.1 = bf16[80,128,256]{2,1,0:T(8,128)(2,1)} custom-call(s32[16,128]{1,0:T(8,128)} %bitcast.14, bf16[160,128,256]{2,1,0:T(8,128)(2,1)} %bitcast.12), custom_call_target="tpu_custom_call" | custom-call | tf_op jit(solution)/shard_map/place/pallas_call | solution.py:374
  (3 shorter events, 0.0 us)
Async XLA Ops:
  2.2 0.7 copy-start
